TPU v7x, 256 devices: a whole 4x4x8 slice. The times are simulated.
256 devices in a mesh: seq: 32 (over x, y, core), head: 8 (over z).
Axes of the slice: x: 4, y: 4, z: 8, core: 2. Of those that a mesh axis runs over, the one named last changes fastest.
Arguments:
- queries: float32 [16384, 1024], P('seq', 'head'), may hold values from -6 to 6
- keys: float32 [16384, 1024], P('seq', 'head'), may hold values from -5 to 5
- values: float32 [16384, 1024], P('seq', 'head'), may hold values from -15 to 15
- gain: float32 [1024], P('head'), may hold values from 0.1 to 1.9
- ridge: float32 [8], P('head'), may hold values from 0.01 to 0.1
- prior_gram: float32 [8, 128, 128], P('head'), as said below
- prior_cross: float32 [8, 128, 128], P('head')
- cotangent: float32 [16384, 1024], P('seq', 'head'), may hold values from -6 to 6
Outputs:
- normed: float32 [16384, 1024], P('seq', 'head')
- grad_queries: float32 [16384, 1024], P('seq', 'head')
- grad_keys: float32 [16384, 1024], P('seq', 'head')
- grad_values: float32 [16384, 1024], P('seq', 'head')
Inputs may be any that keep to these rules, and one draw needn't show every extreme that they name: `prior_gram`: each head's matrix is symmetric positive definite.
All inputs are finite; a program needn't handle non-finite values.
Results may differ from a plain program's by a relative error of at most 0.0003.
Values sent between devices are 32-bit elements; how exact they have to be, the bound alone decides.
A program may use at most 64 MiB of HBM per device.

v0:
```python
import jax
import jax.numpy as jnp
from jax import lax
from jax.sharding import PartitionSpec as P

DH = 128
ITERS = 8
epsilon = 1e-06


def prefix(part, axis, combine, identity, reverse):
    count = lax.axis_size(axis)
    place = lax.axis_index(axis)
    ahead = count - 1 - place if reverse else place
    gathered = jax.tree.map(lambda a: lax.all_gather(a, axis), part)
    state = jax.tree.map(lambda a, e: jnp.zeros_like(a) + jnp.asarray(e, a.dtype), part, identity)

    def one(turn, state):
        source = count - 1 - turn if reverse else turn
        return combine(
            state, jax.tree.map(lambda a: lax.dynamic_index_in_dim(a, source, 0, False), gathered)
        )

    return lax.fori_loop(0, ahead, one, state)


def block_forward(query, keyset, valueset, start_gram, start_cross, ridge_value, first_row):
    highest = lax.Precision.HIGHEST
    count = query.shape[0]
    places = jnp.arange(count)
    causal = (places[None, :] <= places[:, None]).astype(jnp.float32)
    damping = ridge_value * (first_row + places + 1).astype(jnp.float32)[:, None]

    def apply_system(search):
        inner = jnp.dot(search, keyset.T, precision=highest) * causal
        return (
            jnp.dot(search, start_gram, precision=highest)
            + jnp.dot(inner, keyset, precision=highest)
            + damping * search
        )

    def cg_step(carry, unused):
        solution, residual, search, squared = carry
        image = apply_system(search)
        alpha = squared / jnp.sum(search * image, axis=1, keepdims=True)
        solution = solution + alpha * search
        residual = residual - alpha * image
        squared_next = jnp.sum(residual * residual, axis=1, keepdims=True)
        search = residual + squared_next / squared * search
        return ((solution, residual, search, squared_next), None)

    squared = jnp.sum(query * query, axis=1, keepdims=True)
    start = (jnp.zeros_like(query), query, query, squared)
    (solution, _, _, _), _ = lax.scan(cg_step, start, None, length=ITERS)
    inner = jnp.dot(solution, keyset.T, precision=highest) * causal
    return jnp.dot(solution, start_cross, precision=highest) + jnp.dot(
        inner, valueset, precision=highest
    )


def add_pair(earlier, later):
    return (earlier[0] + later[0], earlier[1] + later[1])


def local(queries, keys, values, gain, ridge, prior_gram, prior_cross, cotangent):
    highest = lax.Precision.HIGHEST
    row_count, width = queries.shape
    heads_here = width // DH

    def split_heads(array):
        return array.reshape(row_count, heads_here, DH).transpose(1, 0, 2)

    def join_heads(array):
        return array.transpose(1, 0, 2).reshape(row_count, width)

    head_q = split_heads(queries)
    head_k = split_heads(keys)
    head_v = split_heads(values)
    own_gram = jnp.einsum("hti,htj->hij", head_k, head_k, precision=highest)
    own_cross = jnp.einsum("hti,htj->hij", head_k, head_v, precision=highest)
    position = lax.axis_index("seq")
    first_row = position * row_count
    empty = jnp.zeros_like(own_gram)
    lower_gram, lower_cross = prefix((own_gram, own_cross), "seq", add_pair, (empty, empty), False)
    start_gram = prior_gram + lower_gram
    start_cross = prior_cross + lower_cross
    batched = jax.vmap(jax.checkpoint(block_forward), in_axes=(0, 0, 0, 0, 0, 0, None))

    def local_forward(first, second, third, fourth, fifth):
        return batched(first, second, third, fourth, fifth, ridge, first_row)

    outputs, pullback = jax.vjp(local_forward, head_q, head_k, head_v, start_gram, start_cross)
    mixed = join_heads(outputs)
    scaled_cot = gain * cotangent
    local_square = jnp.sum(mixed * mixed, axis=1)
    local_cross = jnp.sum(scaled_cot * mixed, axis=1)
    total_square = lax.psum(local_square, "head")
    feature_count = width * lax.axis_size("head")
    inverse = lax.rsqrt(total_square / feature_count + epsilon)[:, None]
    normed = mixed * inverse * gain
    total_cross = lax.psum(local_cross, "head")
    grad_mixed = (
        inverse * scaled_cot
        - mixed * (inverse * inverse * inverse) * (total_cross / feature_count)[:, None]
    )
    grad_q, grad_k, grad_v, grad_gram, grad_cross = pullback(split_heads(grad_mixed))
    later_gram, later_cross = prefix((grad_gram, grad_cross), "seq", add_pair, (empty, empty), True)
    symmetric = later_gram + jnp.transpose(later_gram, (0, 2, 1))
    grad_k = (
        grad_k
        + jnp.einsum("hti,hij->htj", head_k, symmetric, precision=highest)
        + jnp.einsum("htj,hij->hti", head_v, later_cross, precision=highest)
    )
    grad_v = grad_v + jnp.einsum("hti,hij->htj", head_k, later_cross, precision=highest)
    return (normed, join_heads(grad_q), join_heads(grad_k), join_heads(grad_v))


def solution(mesh):
    in_specs = (
        P("seq", "head"),
        P("seq", "head"),
        P("seq", "head"),
        P("head"),
        P("head"),
        P("head", None, None),
        P("head", None, None),
        P("seq", "head"),
    )
    out_specs = (P("seq", "head"), P("seq", "head"), P("seq", "head"), P("seq", "head"))
    return jax.shard_map(local, mesh=mesh, in_specs=in_specs, out_specs=out_specs, check_vma=False)
```

profile of v0, /device:TPU:1, one launch (start us, length us, event | category | flops | bytes accessed | tf_op | source)
XLA Modules:
  0.0 445.6 jit_solution(2497507912870803327)
XLA Ops:
  7.2 2.3 fusion.85
  9.7 2.2 fusion.86
  11.9 1.1 copy.57
  13.2 1.1 copy.58
  14.7 49.3 %all-gather.9.cloned.1.call-done = f32[4096,128]{1,0:T(8,128)} async-done(((f32[128,128]{1,0:T(8,128)}), f32[4096,128]{1,0:T(8,128)}) %all-gather.9.cloned.1.call-update) | async-done | bytes 2097168 | tf_op jit(solution)/shard_map/all_gather | solution.py:15
  63.9 51.1 %all-gather.11.cloned.1.call-done = f32[4096,128]{1,0:T(8,128)} async-done(((f32[128,128]{1,0:T(8,128)}), f32[4096,128]{1,0:T(8,128)}) %all-gather.11.cloned.1.call-update) | async-done | bytes 2097168 | tf_op jit(solution)/shard_map/all_gather | solution.py:15
  116.9 30.1 %while.107 = (s32[]{:T(128)}, f32[1,512,128]{1,2,0:T(8,128)S(1)}, f32[1,512,128]{1,2,0:T(8,128)S(1)}, f32[1,512,128]{1,2,0:T(8,128)S(1)}, f32[1,512,1]{1,2,0:T(1...) while((s32[]{:T(128)}, f32[1,512,128]{1,2,0:T(8,128)S(1)}, ...), condition=%wide.region_6.7_spmd.clone, body=%wide.region_3.6_spmd.clone.sunk | while | flops 907675648 | bytes 6125703 | solution.py:54
  117.9 1.2 fusion.135
  121.7 1.2 fusion.135
  125.5 1.2 fusion.135
  129.2 1.2 fusion.135
  133.0 1.2 fusion.135
  136.8 1.2 fusion.135
  140.5 1.2 fusion.135
  144.3 1.2 fusion.135
  148.1 1.2 fusion.87
  149.8 13.8 %all-reduce = (f32[512]{0:T(512)S(1)}, f32[512]{0:T(512)S(1)}) all-reduce(f32[512]{0:T(512)S(1)} %get-tuple-element.1178, f32[512]{0:T(512)S(1)} %get-tuple-element.1177), channel_id=1, replica_groups=mesh['seq'=32,'head'=8] {'head'}, use_global_device_ids=true, to_apply=%region_8.9 | all-reduce | flops 1024 | bytes 8192 | tf_op jit(solution)/shard_map/psum | solution.py:97
  164.9 63.0 %while.108 = (s32[]{:T(128)}, f32[1,512,128]{1,2,0:T(8,128)S(1)}, f32[1,512,128]{1,2,0:T(8,128)S(1)}, f32[1,512,128]{1,2,0:T(8,128)S(1)}, f32[1,512,1]{1,2,0:T(1...) while((s32[]{:T(128)}, f32[1,512,128]{1,2,0:T(8,128)S(1)}, ...), condition=%wide.region_15.16_spmd.clone, body=%wide.region_12.15_spmd.clone.sunk | while | flops 907677696 | bytes 8506591 | solution.py:54
  164.9 2.0 bitcast_dynamic-update-slice_fusion.6
  166.9 1.2 fusion.138
  172.8 2.0 bitcast_dynamic-update-slice_fusion.6
  174.8 1.2 fusion.138
  180.7 2.0 bitcast_dynamic-update-slice_fusion.6
  182.6 1.2 fusion.138
  188.5 2.0 bitcast_dynamic-update-slice_fusion.6
  190.6 1.2 fusion.138
  196.4 2.0 bitcast_dynamic-update-slice_fusion.6
  198.4 1.2 fusion.138
  204.2 2.0 bitcast_dynamic-update-slice_fusion.6
  206.2 1.2 fusion.138
  212.1 2.0 bitcast_dynamic-update-slice_fusion.6
  214.1 1.2 fusion.138
  219.9 2.0 bitcast_dynamic-update-slice_fusion.6
  222.0 1.2 fusion.138
  232.8 99.0 %while.109 = (s32[]{:T(128)}, f32[1,512,128]{1,2,0:T(8,128)S(1)}, f32[1,128,128]{1,2,0:T(8,128)S(1)}, f32[1,512,128]{2,1,0:T(8,128)S(1)}, f32[1,512,128]{2,1,0:T...) while((s32[]{:T(128)}, f32[1,512,128]{1,2,0:T(8,128)S(1)}, ...), condition=%wide.region_20.21_spmd.clone, body=%wide.region_16.20_spmd.clone.sunk | while | flops 1814796800 | bytes 15208740 | solution.py:54
  241.9 2.0 fusion.155
  254.2 2.0 fusion.155
  266.6 2.0 fusion.155
  278.9 2.0 fusion.155
  291.3 2.0 fusion.155
  294.6 1.1 constant_dynamic-slice_fusion.15
  303.7 2.0 fusion.155
  316.1 2.0 fusion.155
  328.5 2.0 fusion.155
  332.7 1.8 copy.75
  337.1 1.8 fusion.64
  339.0 69.1 %all-gather.13.cloned.1.call-done = f32[32,128,128]{2,1,0:T(8,128)} async-done(((f32[1,128,128]{2,1,0:T(8,128)}), f32[32,128,128]{2,1,0:T(8,128)}) %all-gather.13.cloned.1.call-update) | async-done | bytes 2097168 | tf_op jit(solution)/shard_map/all_gather | solution.py:15
  408.1 28.2 %while.106 = (s32[]{:T(128)}, f32[1,128,128]{2,1,0:T(8,128)S(1)}, f32[1,128,128]{2,1,0:T(8,128)S(1)}, s32[]{:T(128)}, f32[32,1,128,128]{3,2,1,0:T(8,128)}, /*ind...) while((s32[]{:T(128)}, f32[1,128,128]{2,1,0:T(8,128)S(1)}, ...), condition=%wide.region_22.23_spmd, body=%wide.region_21.22_spmd.sunk | while | flops 32774 | bytes 393367 | solution.py:24
  (410 shorter events, 182.2 us)
Async XLA Ops:
  7.2 2.5 copy-start
  7.2 7.3 %copy-start.4 = (f32[512,128]{1,0:T(8,128)S(1)}, f32[512,128]{1,0:T(8,128)}, u32[]{:S(2)}) copy-start(f32[512,128]{1,0:T(8,128)} %param.18) | copy-start | bytes 786436
  7.2 7.2 %copy-start.8 = (f32[512,128]{1,0:T(8,128)S(1)}, f32[512,128]{1,0:T(8,128)}, u32[]{:S(2)}) copy-start(f32[512,128]{1,0:T(8,128)} %param.25) | copy-start | bytes 786436
  7.2 56.7 %all-gather.9.cloned.1.call-start = ((), (), s32[]{:S(2)}) async-start(), calls=%async_computation | async-start | bytes 2162688 | tf_op jit(solution)/shard_map/all_gather | solution.py:15
  9.6 105.5 %all-gather.11.cloned.1.call-start = ((), (), s32[]{:S(2)}) async-start(), calls=%async_computation.1 | async-start | bytes 2162688 | tf_op jit(solution)/shard_map/all_gather | solution.py:15
  11.9 327.1 %all-gather.15.cloned.1.call-start = ((), (), s32[]{:S(2)}) async-start(), calls=%async_computation.3 | async-start | bytes 2162688 | tf_op jit(solution)/shard_map/all_gather | solution.py:15
  13.2 103.7 %copy-start.1 = (f32[512,128]{1,0:T(8,128)S(1)}, f32[512,128]{1,0:T(8,128)}, u32[]{:S(2)}) copy-start(f32[512,128]{1,0:T(8,128)} %param.19) | copy-start | bytes 786436
  147.0 2.3 copy-start.10
  147.0 2.3 copy-start.11
  164.4 67.8 %copy-start.6 = (f32[1,512,128]{1,2,0:T(8,128)}, f32[1,512,128]{1,2,0:T(8,128)S(1)}, u32[]{:S(2)}) copy-start(f32[1,512,128]{1,2,0:T(8,128)S(1)} %get-tuple-element.759) | copy-start | bytes 786436
  228.2 4.6 %copy-start.9 = (f32[1,512,1]{1,2,0:T(1,128)S(1)}, f32[1,512,1]{1,2,0:T(1,128)}, u32[]{:S(2)}) copy-start(f32[1,512,1]{1,2,0:T(1,128)} %custom-call.6) | copy-start | bytes 6148
  229.0 179.1 %all-gather.13.cloned.1.call-start = ((), (), s32[]{:S(2)}) async-start(), calls=%async_computation.2 | async-start | bytes 2162688 | tf_op jit(solution)/shard_map/all_gather | solution.py:15
  230.2 1.0 copy-start.2
  331.8 3.7 copy-start.7
  332.6 3.7 copy-start.5
  334.5 2.6 copy-start.3
Sparse Core Ops, SparseCore 0:
  11.1 52.7 all-gather.8
  67.1 47.9 all-gather.10
  229.1 75.3 all-gather.14
  332.7 75.3 all-gather.12
where the time goes:
time: 449 us; the launch traced here: 446 us
  waiting for transfers between devices  170 us (38%)
  matrix products  112 us (25%)
  other arithmetic  89.9 us (20%)
  local copies, waits for them, and re-layouts  42.8 us (10%)
  between operations  14.3 us (3%)
  blocking collectives  13.8 us (3%)
    all_gather x4, waiting for transfers between devices, prefix(): gathered = jax.tree.map(lambda a: lax.all_gather(a, axis), part)  169 us
    dot_general x32, matrix products, apply_system(): jnp.dot(inner, keyset, precision=highest)  43.5 us
    dot_general x32, matrix products, apply_system(): inner = jnp.dot(search, keyset.T, precision=highest) * causal  38 us
    dynamic_slice x56, local copies, waits for them, and re-layouts, block_forward(): (solution, _, _, _), _ = lax.scan(cg_step, start, None, length=ITERS)  30.2 us
    add x31, other arithmetic, add_pair(): return (earlier[0] + later[0], earlier[1] + later[1])  28.2 us
    dynamic_update_slice x32, other arithmetic, block_forward(): (solution, _, _, _), _ = lax.scan(cg_step, start, None, length=ITERS)  21.7 us
    mul x24, other arithmetic, block_forward(): ridge_value * (first_row + places + 1).astype(jnp.float32)[:, None]  15.7 us
    dot_general x32, matrix products, apply_system(): jnp.dot(search, start_gram, precision=highest)  15.3 us
  transfers between devices with their start and end apart: 4, of which 3 were waited for; matrix products, arithmetic and copies ran while one was open for 25% of the time, Pallas kernels for 0%

commit v1 on v0

--- a/solution.py
+++ b/solution.py
@@ -94,7 +94,8 @@
     scaled_cot = gain * cotangent
     local_square = jnp.sum(mixed * mixed, axis=1)
     local_cross = jnp.sum(scaled_cot * mixed, axis=1)
-    total_square = lax.psum(local_square, "head")
+    blocks = lax.all_gather(local_square, "head")
+    total_square = jnp.sum(blocks, axis=0)
     feature_count = width * lax.axis_size("head")
     inverse = lax.rsqrt(total_square / feature_count + epsilon)[:, None]
     normed = mixed * inverse * gain

time: 449 us -> 470 us (1.047)
  blocking collectives: 13.8 us -> 29.2 us
  waiting for transfers between devices: 170 us -> 175 us
    all_gather x0 -> x1, blocking collectives: none -> 18.4 us  [local(): blocks = lax.all_gather(local_square, 'head')]
    all_gather x4, waiting for transfers between devices: 169 us -> 175 us  [prefix(): gathered = jax.tree.map(lambda a: lax.all_gather(a, axis), part)]
  transfers between devices with their start and end apart: 4 -> 4, of which waited for: 3 -> 3; matrix products, arithmetic and copies ran while one was open for 25% -> 24% of each run, Pallas kernels for 0% -> 0%
where the time goes in v1:
time: 470 us; the launch traced here: 467 us
  waiting for transfers between devices  175 us (37%)
  matrix products  112 us (24%)
  other arithmetic  89.9 us (19%)
  local copies, waits for them, and re-layouts  42.9 us (9%)
  blocking collectives  29.2 us (6%)
  between operations  14.3 us (3%)
    all_gather x4, waiting for transfers between devices, prefix(): gathered = jax.tree.map(lambda a: lax.all_gather(a, axis), part)  175 us
    dot_general x32, matrix products, apply_system(): jnp.dot(inner, keyset, precision=highest)  43.5 us
    dot_general x32, matrix products, apply_system(): inner = jnp.dot(search, keyset.T, precision=highest) * causal  38 us
    dynamic_slice x56, local copies, waits for them, and re-layouts, block_forward(): (solution, _, _, _), _ = lax.scan(cg_step, start, None, length=ITERS)  30.1 us
    add x31, other arithmetic, add_pair(): return (earlier[0] + later[0], earlier[1] + later[1])  28.2 us
    dynamic_update_slice x32, other arithmetic, block_forward(): (solution, _, _, _), _ = lax.scan(cg_step, start, None, length=ITERS)  21.7 us
    all_gather x1, blocking collectives, local(): blocks = lax.all_gather(local_square, 'head')  18.4 us
    mul x24, other arithmetic, block_forward(): ridge_value * (first_row + places + 1).astype(jnp.float32)[:, None]  15.7 us
  transfers between devices with their start and end apart: 4, of which 3 were waited for; matrix products, arithmetic and copies ran while one was open for 24% of the time, Pallas kernels for 0%

profile of v1, /device:TPU:1, one launch (start us, length us, event | category | flops | bytes accessed | tf_op | source)
XLA Modules:
  0.0 466.7 jit_solution(14232697312443214898)
XLA Ops:
  7.2 2.3 fusion.85
  9.7 2.2 fusion.86
  11.9 1.1 copy.57
  13.2 1.1 copy.58
  14.7 49.3 %all-gather.11.cloned.1.call-done = f32[4096,128]{1,0:T(8,128)} async-done(((f32[128,128]{1,0:T(8,128)}), f32[4096,128]{1,0:T(8,128)}) %all-gather.11.cloned.1.call-update) | async-done | bytes 2097168 | tf_op jit(solution)/shard_map/all_gather | solution.py:15
  63.9 51.1 %all-gather.13.cloned.1.call-done = f32[4096,128]{1,0:T(8,128)} async-done(((f32[128,128]{1,0:T(8,128)}), f32[4096,128]{1,0:T(8,128)}) %all-gather.13.cloned.1.call-update) | async-done | bytes 2097168 | tf_op jit(solution)/shard_map/all_gather | solution.py:15
  116.9 30.1 %while.107 = (s32[]{:T(128)}, f32[1,512,128]{1,2,0:T(8,128)S(1)}, f32[1,512,128]{1,2,0:T(8,128)S(1)}, f32[1,512,128]{1,2,0:T(8,128)S(1)}, f32[1,512,1]{1,2,0:T(1...) while((s32[]{:T(128)}, f32[1,512,128]{1,2,0:T(8,128)S(1)}, ...), condition=%wide.region_6.7_spmd.clone, body=%wide.region_3.6_spmd.clone.sunk | while | flops 907675648 | bytes 6125703 | solution.py:54
  117.9 1.2 fusion.135
  121.7 1.2 fusion.135
  125.5 1.2 fusion.135
  129.2 1.2 fusion.135
  133.0 1.2 fusion.135
  136.8 1.2 fusion.135
  140.5 1.2 fusion.135
  144.3 1.2 fusion.135
  148.1 1.2 fusion.87
  149.8 18.4 %all-gather.5 = f32[8,1,512]{2,1,0:T(1,128)S(1)} all-gather(f32[1,1,512]{2,1,0:T(1,128)S(1)} %bitcast.515), channel_id=4, replica_groups=mesh['seq'=32,'head'=8] {'head'}, dimensions={0}, use_global_device_ids=true | all-gather | bytes 18432 | tf_op jit(solution)/shard_map/all_gather | solution.py:97
  168.2 10.9 %psum.7 = f32[512]{0:T(512)S(1)} all-reduce(f32[512]{0:T(512)S(1)} %get-tuple-element.1177), channel_id=1, replica_groups=mesh['seq'=32,'head'=8] {'head'}, use_global_device_ids=true, to_apply=%region_10.11 | all-reduce | flops 512 | bytes 4096 | tf_op jit(solution)/shard_map/psum | solution.py:102
  180.3 63.0 %while.108 = (s32[]{:T(128)}, f32[1,512,128]{1,2,0:T(8,128)S(1)}, f32[1,512,128]{1,2,0:T(8,128)S(1)}, f32[1,512,128]{1,2,0:T(8,128)S(1)}, f32[1,512,1]{1,2,0:T(1...) while((s32[]{:T(128)}, f32[1,512,128]{1,2,0:T(8,128)S(1)}, ...), condition=%wide.region_15.16_spmd.clone, body=%wide.region_12.15_spmd.clone.sunk | while | flops 907677696 | bytes 8506591 | solution.py:54
  180.4 2.0 bitcast_dynamic-update-slice_fusion.6
  182.4 1.2 fusion.138
  188.2 2.0 bitcast_dynamic-update-slice_fusion.6
  190.3 1.2 fusion.138
  196.1 2.0 bitcast_dynamic-update-slice_fusion.6
  198.1 1.2 fusion.138
  204.0 2.0 bitcast_dynamic-update-slice_fusion.6
  206.0 1.2 fusion.138
  211.9 2.0 bitcast_dynamic-update-slice_fusion.6
  213.9 1.2 fusion.138
  219.7 2.0 bitcast_dynamic-update-slice_fusion.6
  221.7 1.2 fusion.138
  227.6 2.0 bitcast_dynamic-update-slice_fusion.6
  229.6 1.2 fusion.138
  235.4 2.0 bitcast_dynamic-update-slice_fusion.6
  237.5 1.2 fusion.138
  248.4 98.9 %while.109 = (s32[]{:T(128)}, f32[1,512,128]{1,2,0:T(8,128)S(1)}, f32[1,128,128]{1,2,0:T(8,128)S(1)}, f32[1,512,128]{2,1,0:T(8,128)S(1)}, f32[1,512,128]{2,1,0:T...) while((s32[]{:T(128)}, f32[1,512,128]{1,2,0:T(8,128)S(1)}, ...), condition=%wide.region_20.21_spmd.clone, body=%wide.region_16.20_spmd.clone.sunk | while | flops 1814796800 | bytes 15208740 | solution.py:54
  257.4 2.0 fusion.155
  269.8 2.0 fusion.155
  282.1 2.0 fusion.155
  294.5 2.0 fusion.155
  306.8 2.0 fusion.155
  319.2 2.0 fusion.155
  331.6 2.0 fusion.155
  343.9 2.0 fusion.155
  348.2 1.8 copy.75
  352.6 1.8 fusion.64
  354.5 74.7 %all-gather.15.cloned.1.call-done = f32[32,128,128]{2,1,0:T(8,128)} async-done(((f32[1,128,128]{2,1,0:T(8,128)}), f32[32,128,128]{2,1,0:T(8,128)}) %all-gather.15.cloned.1.call-update) | async-done | bytes 2097168 | tf_op jit(solution)/shard_map/all_gather | solution.py:15
  429.2 28.2 %while.106 = (s32[]{:T(128)}, f32[1,128,128]{2,1,0:T(8,128)S(1)}, f32[1,128,128]{2,1,0:T(8,128)S(1)}, s32[]{:T(128)}, f32[32,1,128,128]{3,2,1,0:T(8,128)}, /*ind...) while((s32[]{:T(128)}, f32[1,128,128]{2,1,0:T(8,128)S(1)}, ...), condition=%wide.region_22.23_spmd, body=%wide.region_21.22_spmd.sunk | while | flops 32774 | bytes 393367 | solution.py:24
  (413 shorter events, 183.3 us)
Async XLA Ops:
  7.2 2.5 copy-start
  7.2 7.3 %copy-start.4 = (f32[512,128]{1,0:T(8,128)S(1)}, f32[512,128]{1,0:T(8,128)}, u32[]{:S(2)}) copy-start(f32[512,128]{1,0:T(8,128)} %param.18) | copy-start | bytes 786436
  7.2 7.2 %copy-start.8 = (f32[512,128]{1,0:T(8,128)S(1)}, f32[512,128]{1,0:T(8,128)}, u32[]{:S(2)}) copy-start(f32[512,128]{1,0:T(8,128)} %param.25) | copy-start | bytes 786436
  7.2 56.7 %all-gather.11.cloned.1.call-start = ((), (), s32[]{:S(2)}) async-start(), calls=%async_computation | async-start | bytes 2162688 | tf_op jit(solution)/shard_map/all_gather | solution.py:15
  9.6 105.5 %all-gather.13.cloned.1.call-start = ((), (), s32[]{:S(2)}) async-start(), calls=%async_computation.1 | async-start | bytes 2162688 | tf_op jit(solution)/shard_map/all_gather | solution.py:15
  11.9 342.6 %all-gather.17.cloned.1.call-start = ((), (), s32[]{:S(2)}) async-start(), calls=%async_computation.3 | async-start | bytes 2162688 | tf_op jit(solution)/shard_map/all_gather | solution.py:15
  13.2 103.7 %copy-start.1 = (f32[512,128]{1,0:T(8,128)S(1)}, f32[512,128]{1,0:T(8,128)}, u32[]{:S(2)}) copy-start(f32[512,128]{1,0:T(8,128)} %param.19) | copy-start | bytes 786436
  147.0 2.3 copy-start.10
  147.0 2.3 copy-start.11
  179.9 67.9 %copy-start.6 = (f32[1,512,128]{1,2,0:T(8,128)}, f32[1,512,128]{1,2,0:T(8,128)S(1)}, u32[]{:S(2)}) copy-start(f32[1,512,128]{1,2,0:T(8,128)S(1)} %get-tuple-element.759) | copy-start | bytes 786436
  243.8 4.6 copy-start.9
  244.5 184.7 %all-gather.15.cloned.1.call-start = ((), (), s32[]{:S(2)}) async-start(), calls=%async_computation.2 | async-start | bytes 2162688 | tf_op jit(solution)/shard_map/all_gather | solution.py:15
  245.8 1.0 copy-start.2
  347.3 3.7 copy-start.7
  348.1 3.7 copy-start.5
  350.0 2.6 copy-start.3
Sparse Core Ops, SparseCore 0:
  11.1 52.7 all-gather.10
  67.1 47.9 all-gather.12
  244.6 80.9 all-gather.16
  348.2 80.9 all-gather.14
